TPU v7x, 32 devices: a whole 2x2x4 slice. The times are simulated.
32 devices in a mesh: seq: 2 (over x), fsdp: 16 (over z, y, core).
Axes of the slice: x: 2, y: 2, z: 4, core: 2. Of those that a mesh axis runs over, the one named last changes fastest.
Arguments:
- residual_in: bfloat16 [16, 1024, 767], P('fsdp', 'seq'), may hold values from -6 to 6
- cotangent: bfloat16 [16, 1024, 767], P('fsdp', 'seq'), may hold values from -6 to 6
- w_qkv: bfloat16 [768, 2304], P('fsdp'), may hold values from -0.3125 to 0.3125
- w_out: bfloat16 [768, 768], P('fsdp'), may hold values from -1.25 to 1.25
- w_fc: bfloat16 [768, 3072], P('fsdp'), may hold values from -0.21875 to 0.21875
- w_proj: bfloat16 [3072, 768], P('fsdp'), may hold values from -0.109375 to 0.109375
- attn_bias: bfloat16 [3, 768], P(None, 'fsdp'), may hold values from -1.5 to 1.5
- fc_bias: bfloat16 [3072], P('fsdp'), may hold values from -1.5 to 1.5
- proj_bias: bfloat16 [768], P('fsdp'), may hold values from -1.5 to 1.5
- gains: bfloat16 [2, 768], P(None, 'fsdp'), may hold values from 0.099609375 to 1.8984375
Outputs:
- residual_out: bfloat16 [16, 1024, 767], P('fsdp', 'seq')
- input_grad: bfloat16 [16, 1024, 767], P('fsdp', 'seq')
- grad_qkv: float32 [768, 2304], P('fsdp')
- grad_out: float32 [768, 768], P('fsdp')
- grad_fc: float32 [768, 3072], P('fsdp')
- grad_proj: float32 [3072, 768], P('fsdp')
- grad_attn_bias: float32 [3, 768], P(None, 'fsdp')
- grad_fc_bias: float32 [3072], P('fsdp')
- grad_proj_bias: float32 [768], P('fsdp')
- grad_gains: float32 [2, 768], P(None, 'fsdp')
All inputs are finite; a program needn't handle non-finite values.
Results may differ from a plain program's by a relative error of at most 0.014.
The roundings to bfloat16 on the way count: a program that leaves them out, or rounds other values in their place, can miss the bound.
Values may be sent and summed in bfloat16 or wider, within the bound.
A program may use at most 192 MiB of HBM per device.

v0:
```python
import jax
import jax.numpy as jnp
from jax import lax
from jax.sharding import PartitionSpec as P

HD = 64


EPSILON = 1e-05
MASKED = -1e30


def rms_norm(values, gain):
    return values * lax.rsqrt(jnp.mean(values * values, axis=-1, keepdims=True) + EPSILON) * gain


def center(values):
    return values - jnp.mean(values, axis=-1, keepdims=True)


def gelu_tanh(values):
    return jax.nn.gelu(values, approximate=True)


def matmul(left, right):
    return jnp.dot(left, right, preferred_element_type=jnp.float32)


def weight_grad(inputs, grads):
    return lax.dot_general(
        inputs, grads, (((0,), (0,)), ((), ())), preferred_element_type=jnp.float32
    )


def input_grad_of(grads, weight):
    return lax.dot_general(
        grads, weight, (((1,), (1,)), ((), ())), preferred_element_type=jnp.float32
    )


def block_rows(length):
    return min(length, max(512, length // 8))


def score_block(query_block, keys_part, start, scale):
    scores = (
        jnp.einsum("qhd,khd->hqk", query_block, keys_part, preferred_element_type=jnp.float32)
        * scale
    )
    query_pos = start + jnp.arange(query_block.shape[0], dtype=jnp.int32)
    key_pos = jnp.arange(keys_part.shape[0], dtype=jnp.int32)
    allowed = query_pos[:, None] >= key_pos[None, :]
    return jnp.where(allowed[None], scores, MASKED)


def attend(queries, keys_all, values_all, scale):
    length, head_count, width = queries.shape
    block = block_rows(length)
    count = length // block
    results = []
    log_totals = []
    for index in range(count):
        start = index * block
        finish = start + block
        scores = score_block(queries[start:finish], keys_all[:finish], start, scale)
        peak = jnp.max(scores, axis=-1, keepdims=True)
        weights = jnp.exp(scores - peak)
        total = jnp.sum(weights, axis=-1, keepdims=True)
        weights = weights / total
        result = jnp.einsum(
            "hqk,khd->qhd",
            weights.astype(jnp.bfloat16),
            values_all[:finish],
            preferred_element_type=jnp.float32,
        )
        results.append(result.astype(jnp.bfloat16))
        log_totals.append((peak + jnp.log(total))[..., 0])
    joined = jnp.concatenate(results, axis=0)
    return (joined.reshape(length, head_count * width), log_totals)


def attend_back(queries, keys_all, values_all, log_totals, grad_heads, scale):
    length, head_count, width = queries.shape
    block = block_rows(length)
    count = length // block
    key_sum = jnp.zeros((length, head_count, width), jnp.float32)
    value_sum = jnp.zeros((length, head_count, width), jnp.float32)
    query_grads = []
    for index in range(count):
        start = index * block
        finish = start + block
        query_block = queries[start:finish]
        grad_block = grad_heads[start:finish]
        keys_part = keys_all[:finish]
        scores = score_block(query_block, keys_part, start, scale)
        weights = jnp.exp(scores - log_totals[index][..., None])
        grad_weights = jnp.einsum(
            "qhd,khd->hqk", grad_block, values_all[:finish], preferred_element_type=jnp.float32
        )
        inner = jnp.sum(weights * grad_weights, axis=-1, keepdims=True)
        grad_scores = (weights * (grad_weights - inner)).astype(jnp.bfloat16)
        query_grad = (
            jnp.einsum("hqk,khd->qhd", grad_scores, keys_part, preferred_element_type=jnp.float32)
            * scale
        )
        key_part = (
            jnp.einsum("hqk,qhd->khd", grad_scores, query_block, preferred_element_type=jnp.float32)
            * scale
        )
        value_part = jnp.einsum(
            "hqk,qhd->khd",
            weights.astype(jnp.bfloat16),
            grad_block,
            preferred_element_type=jnp.float32,
        )
        key_sum = key_sum.at[:finish].add(key_part)
        value_sum = value_sum.at[:finish].add(value_part)
        query_grads.append(query_grad.astype(jnp.bfloat16))
    return (
        jnp.concatenate(query_grads, axis=0),
        key_sum.astype(jnp.bfloat16),
        value_sum.astype(jnp.bfloat16),
    )


def local(residual_in, cotangent, w_qkv, w_out, w_fc, w_proj, attn_bias, fc_bias, proj_bias, gains):
    seq_count = lax.axis_size("seq")
    tok_rows = residual_in.shape[1]
    model_width = w_qkv.shape[1] // 3
    share = model_width // seq_count
    head_count = share // HD
    scale = HD ** (-0.5)
    compact = residual_in[0].astype(jnp.float32)
    full = jnp.concatenate([compact, -jnp.sum(compact, axis=-1, keepdims=True)], axis=-1)
    qkv_w, out_w, attn_b, gain_w = (
        lax.all_gather(w_qkv, "fsdp", axis=0, tiled=True),
        lax.all_gather(w_out, "fsdp", axis=0, tiled=True),
        lax.all_gather(attn_bias, "fsdp", axis=1, tiled=True),
        lax.all_gather(gains, "fsdp", axis=1, tiled=True),
    )
    gain_all = gain_w.astype(jnp.float32)
    bias_all = attn_b.astype(jnp.float32)
    normed = rms_norm(full, gain_all[0]).astype(jnp.bfloat16)
    bias_qkv = jnp.concatenate([bias_all[0], jnp.zeros_like(bias_all[0]), bias_all[1]])
    projected = (matmul(normed, qkv_w) + bias_qkv).astype(jnp.bfloat16)
    by_heads = lax.all_to_all(
        projected.reshape(tok_rows, 3, seq_count, share),
        "seq",
        split_axis=2,
        concat_axis=0,
        tiled=True,
    )
    length = by_heads.shape[0]
    queries = by_heads[:, 0, 0].reshape(length, head_count, HD)
    keys_all = by_heads[:, 1, 0].reshape(length, head_count, HD)
    values_all = by_heads[:, 2, 0].reshape(length, head_count, HD)
    attended, log_totals = attend(queries, keys_all, values_all, scale)
    mixed = lax.all_to_all(
        attended.reshape(length, 1, share), "seq", split_axis=0, concat_axis=1, tiled=True
    )
    mixed = mixed.reshape(tok_rows, model_width)
    branch = matmul(mixed, out_w) + bias_all[2]
    middle = full + center(branch)
    fc_w, proj_w, fc_b, proj_b = (
        lax.all_gather(w_fc, "fsdp", axis=0, tiled=True),
        lax.all_gather(w_proj, "fsdp", axis=0, tiled=True),
        lax.all_gather(fc_bias, "fsdp", axis=0, tiled=True),
        lax.all_gather(proj_bias, "fsdp", axis=0, tiled=True),
    )
    normed_two = rms_norm(middle, gain_all[1]).astype(jnp.bfloat16)
    hidden = matmul(normed_two, fc_w) + fc_b.astype(jnp.float32)
    activated = gelu_tanh(hidden).astype(jnp.bfloat16)
    branch_two = matmul(activated, proj_w) + proj_b.astype(jnp.float32)
    final = middle + center(branch_two)
    residual_out = final[:, :-1].astype(jnp.bfloat16)[None]
    qkv_w, out_w, fc_w, proj_w, gain_w = (
        lax.all_gather(w_qkv, "fsdp", axis=0, tiled=True),
        lax.all_gather(w_out, "fsdp", axis=0, tiled=True),
        lax.all_gather(w_fc, "fsdp", axis=0, tiled=True),
        lax.all_gather(w_proj, "fsdp", axis=0, tiled=True),
        lax.all_gather(gains, "fsdp", axis=1, tiled=True),
    )
    gain_all = gain_w.astype(jnp.float32)
    upstream = cotangent[0].astype(jnp.float32)
    grad_final = jnp.concatenate([upstream, jnp.zeros((tok_rows, 1), jnp.float32)], axis=-1)
    grad_branch_two = center(grad_final).astype(jnp.bfloat16)
    grad_proj = weight_grad(activated, grad_branch_two)
    grad_proj_bias = jnp.sum(grad_branch_two.astype(jnp.float32), axis=0)
    grad_activated = input_grad_of(grad_branch_two, proj_w)
    gelu_pull = jax.vjp(gelu_tanh, hidden)[1]
    grad_hidden = gelu_pull(grad_activated)[0].astype(jnp.bfloat16)
    grad_fc = weight_grad(normed_two, grad_hidden)
    grad_fc_bias = jnp.sum(grad_hidden.astype(jnp.float32), axis=0)
    grad_normed_two = input_grad_of(grad_hidden, fc_w)
    second_pull = jax.vjp(rms_norm, middle, gain_all[1])[1]
    grad_middle_norm, grad_gain_two = second_pull(grad_normed_two)
    grad_middle = grad_final + grad_middle_norm
    grad_branch = center(grad_middle).astype(jnp.bfloat16)
    grad_out = weight_grad(mixed, grad_branch)
    grad_out_bias = jnp.sum(grad_branch.astype(jnp.float32), axis=0)
    grad_mixed = input_grad_of(grad_branch, out_w).astype(jnp.bfloat16)
    grad_heads = lax.all_to_all(
        grad_mixed.reshape(tok_rows, seq_count, share),
        "seq",
        split_axis=1,
        concat_axis=0,
        tiled=True,
    )
    grad_heads = grad_heads.reshape(length, head_count, HD)
    grad_queries, grad_keys, grad_values = attend_back(
        queries, keys_all, values_all, log_totals, grad_heads, scale
    )
    stacked = jnp.stack([grad_queries, grad_keys, grad_values], axis=1).reshape(length, 3, 1, share)
    grad_projected = lax.all_to_all(stacked, "seq", split_axis=0, concat_axis=2, tiled=True)
    grad_projected = grad_projected.reshape(tok_rows, 3 * model_width)
    grad_qkv = weight_grad(normed, grad_projected)
    column_sums = jnp.sum(grad_projected.astype(jnp.float32), axis=0)
    grad_attn_bias = jnp.stack(
        [column_sums[:model_width], column_sums[2 * model_width :], grad_out_bias]
    )
    grad_normed = input_grad_of(grad_projected, qkv_w)
    first_pull = jax.vjp(rms_norm, full, gain_all[0])[1]
    grad_full_norm, grad_gain_one = first_pull(grad_normed)
    grad_full = grad_middle + grad_full_norm
    input_grad = (grad_full[:, :-1] - grad_full[:, -1:]).astype(jnp.bfloat16)[None]
    shards = (
        lax.psum_scatter(grad_qkv, "fsdp", scatter_dimension=0, tiled=True),
        lax.psum_scatter(grad_out, "fsdp", scatter_dimension=0, tiled=True),
        lax.psum_scatter(grad_fc, "fsdp", scatter_dimension=0, tiled=True),
        lax.psum_scatter(grad_proj, "fsdp", scatter_dimension=0, tiled=True),
        lax.psum_scatter(grad_attn_bias, "fsdp", scatter_dimension=1, tiled=True),
        lax.psum_scatter(grad_fc_bias, "fsdp", scatter_dimension=0, tiled=True),
        lax.psum_scatter(grad_proj_bias, "fsdp", scatter_dimension=0, tiled=True),
        lax.psum_scatter(
            jnp.stack([grad_gain_one, grad_gain_two]), "fsdp", scatter_dimension=1, tiled=True
        ),
    )
    totals = (
        lax.psum(shards[0].astype(jnp.bfloat16), "seq").astype(jnp.float32),
        lax.psum(shards[1].astype(jnp.bfloat16), "seq").astype(jnp.float32),
        lax.psum(shards[2].astype(jnp.bfloat16), "seq").astype(jnp.float32),
        lax.psum(shards[3].astype(jnp.bfloat16), "seq").astype(jnp.float32),
        lax.psum(shards[4].astype(jnp.bfloat16), "seq").astype(jnp.float32),
        lax.psum(shards[5].astype(jnp.bfloat16), "seq").astype(jnp.float32),
        lax.psum(shards[6].astype(jnp.bfloat16), "seq").astype(jnp.float32),
        lax.psum(shards[7].astype(jnp.bfloat16), "seq").astype(jnp.float32),
    )
    return (
        residual_out,
        input_grad,
        totals[0],
        totals[1],
        totals[2],
        totals[3],
        totals[4],
        totals[5],
        totals[6],
        totals[7],
    )


def solution(mesh):
    in_specs = (
        P("fsdp", "seq", None),
        P("fsdp", "seq", None),
        P("fsdp", None),
        P("fsdp", None),
        P("fsdp", None),
        P("fsdp", None),
        P(None, "fsdp"),
        P("fsdp"),
        P("fsdp"),
        P(None, "fsdp"),
    )
    out_specs = (
        P("fsdp", "seq", None),
        P("fsdp", "seq", None),
        P("fsdp", None),
        P("fsdp", None),
        P("fsdp", None),
        P("fsdp", None),
        P(None, "fsdp"),
        P("fsdp"),
        P("fsdp"),
        P(None, "fsdp"),
    )
    return jax.shard_map(local, mesh=mesh, in_specs=in_specs, out_specs=out_specs, check_vma=False)
```

profile of v0, /device:TPU:0, one launch (start us, length us, event | category | flops | bytes accessed | tf_op | source)
XLA Modules:
  0.0 865.7 jit_solution(10618196330818193534)
XLA Ops:
  12.6 23.0 %all-gather = bf16[16,48,2]{1,2,0:T(2,128)(2,1)S(1)} all-gather(bf16[1,48,2]{1,2,0:T(2,128)(2,1)S(1)} %bitcast.172), channel_id=1, replica_groups=mesh['seq'=2,'fsdp'=16] {'fsdp'}, dimensions={0}, use_global_device_ids=true | all-gather | bytes 3264 | tf_op jit(solution)/shard_map/all_gather | solution.py:139
  35.7 17.7 %all-gather.1 = bf16[16,48,3]{1,2,0:T(4,128)(2,1)S(1)} all-gather(bf16[1,48,3]{1,2,0:T(4,128)(2,1)S(1)} %bitcast.171), channel_id=1, replica_groups=mesh['seq'=2,'fsdp'=16] {'fsdp'}, dimensions={0}, use_global_device_ids=true | all-gather | bytes 4896 | tf_op jit(solution)/shard_map/all_gather | solution.py:138
  54.0 6.3 all-gather.7.cloned.1.call-done
  60.3 5.5 fusion.15
  65.8 5.6 reshape.310
  71.4 3.4 copy.92
  74.8 5.4 all-to-all-start
  82.2 26.4 %all-to-all-done = bf16[512,3,2,384]{3,0,1,2:T(8,128)(2,1)} async-done(((bf16[512,3,2,384]{3,0,1,2:T(8,128)(2,1)}), bf16[512,3,2,384]{3,0,1,2:T(8,128)(2,1)}, u32[]{:S(2)}, u32[]{:S(2)}) %all-to-all-start) | async-done | bytes 2359328 | tf_op jit(solution)/shard_map/all_to_all | solution.py:146
  113.4 2.7 fusion.54
  126.6 2.4 fusion.58
  129.0 2.8 fusion
  133.6 3.3 fusion.38
  140.2 4.3 all-to-all-start.1
  147.0 32.4 %all-reduce.8 = (bf16[768]{0:T(1024)(128)(2,1)S(1)}, bf16[3072]{0:T(1024)(128)(2,1)S(1)}) all-reduce(bf16[768]{0:T(1024)(128)(2,1)S(1)} %dynamic-update-slice.11, bf16[3072]{0:T(1024)(128)(2,1)S(1)} %dynamic-update-slice.10), channel_id=1, replica_groups=mesh['seq'=2,'fsdp'=16] {'fsdp'}, use_global_device_ids=true, to_apply=%add.4 | all-reduce | flops 3840 | bytes 15360
  184.0 2.4 fusion.60
  187.0 7.6 fusion.46
  194.6 14.2 %all-gather.13.cloned.1.call-done = bf16[3072,768]{1,0:T(8,128)(2,1)} async-done(((bf16[192,768]{1,0:T(8,128)(2,1)}), bf16[3072,768]{1,0:T(8,128)(2,1)}) %all-gather.13.cloned.1.call-update) | async-done | bytes 4718608 | tf_op jit(solution)/shard_map/all_gather | solution.py:166
  208.8 9.3 %convert_reduce_fusion = (f32[3072]{0:T(1024)S(1)}, bf16[512,3072]{1,0:T(8,128)(2,1)S(1)}) fusion(f32[512,3072]{1,0:T(8,128)} %fusion.46, f32[3072]{0:T(1024)S(1)} %convert_element_type.173, bf16[3072,768]{1,0:T(8,128)(2,1)} %all-gather.13.cloned.1.call-done, f32[512]{0:T(512)S(1)} %get-tuple-element.131, bf16[512,767]{1,0:T(8,128)(2,1)S(1)} %bitcast.154), kind=kOutput, calls=%fused_computation.18 | convolution fusion | flops 2453271552 | bytes 14967808 | tf_op jit(solution)/shard_map/dot_general | solution.py:36
  218.1 2.9 multiply_reduce_fusion.2
  224.1 3.5 all-to-all-start.2
  230.1 8.9 %all-to-all-done.2 = bf16[512,2,384]{2,0,1:T(8,128)(2,1)S(1)} async-done(((bf16[512,2,384]{2,0,1:T(8,128)(2,1)}), bf16[512,2,384]{2,0,1:T(8,128)(2,1)S(1)}, u32[]{:S(2)}, u32[]{:S(2)}) %all-to-all-start.2) | async-done | bytes 786464 | tf_op jit(solution)/shard_map/all_to_all | solution.py:202
  240.1 5.0 fusion.28
  245.1 7.0 multiply_reduce_fusion.1
  254.1 10.1 %multiply_reduce_fusion = (f32[6,512]{1,0:T(8,128)S(1)}, f32[6,512,1024]{2,1,0:T(8,128)}) fusion(f32[6,512,1024]{2,1,0:T(8,128)} %copy-done, f32[6,512]{1,0:T(8,128)S(1)} %log_add_fusion, bf16[512,6,64]{0,2,1:T(8,128)(2,1)} %bitcast.144, bf16[1024,6,64]{0,2,1:T(8,128)(2,1)} %bitcast.146), kind=kOutput, calls=%fused_computation.1 | convolution fusion | flops 412087296 | bytes 26370048 | tf_op jit(solution)/shard_map/qhd,khd->hqk/dot_general | solution.py:97
  264.1 7.0 fusion.24
  271.2 6.4 multiply_convert_fusion.1
  277.6 9.6 %multiply_convert_fusion = bf16[6,512,1024]{2,1,0:T(8,128)(2,1)} fusion(f32[6,512,1024]{2,1,0:T(8,128)} %get-tuple-element.126, f32[6,512,1024]{2,1,0:T(8,128)S(1)} %bitcast.122, f32[6,512]{1,0:T(8,128)S(1)} %get-tuple-element.125, f32[6,512]{1,0:T(8,128)S(1)} %log_add_fusion), kind=kLoop, calls=%fused_computation | loop fusion | flops 12582912 | bytes 31481856 | tf_op jit(solution)/shard_map/convert_element_type | solution.py:101
  289.1 4.8 copy.111
  294.0 5.1 fusion.25
  299.1 4.8 copy.110
  305.7 4.8 fusion.37
  311.5 5.1 copy.109
  316.6 6.8 pad_maximum_fusion
  323.4 38.6 %all_to_all.63 = bf16[1024,3,1,384]{3,1,2,0:T(4,128)(2,1)S(1)} all-to-all(bf16[1024,3,1,384]{3,1,2,0:T(4,128)(2,1)S(1)} %pad_maximum_fusion), channel_id=1, replica_groups=mesh['seq'=2,'fsdp'=16] {'seq'}, dimensions={0} | all-to-all | bytes 4718592 | tf_op jit(solution)/shard_map/all_to_all | solution.py:214
  363.7 4.4 copy.113
  368.2 6.8 fusion.44
  376.1 10.7 %fusion.47 = f32[3072,768]{1,0:T(8,128)} fusion(f32[512]{0:T(512)S(1)} %get-tuple-element.131, bf16[512,767]{1,0:T(8,128)(2,1)S(1)} %bitcast.156, f32[512,3072]{1,0:T(8,128)} %fusion.46, f32[3072]{0:T(1024)S(1)} %convert_element_type.173), kind=kOutput, calls=%fused_computation.122 | convolution fusion | flops 2432827392 | bytes 16528384 | tf_op jit(solution)/shard_map/dot_general | solution.py:30
  388.4 7.4 fusion.45
  397.4 9.4 %fusion.61 = (f32[512]{0:T(512)S(1)}, f32[512,768]{1,0:T(8,128)}) fusion(f32[768]{0:T(1024)S(1)} %convert_element_type.175, bf16[3072,768]{1,0:T(8,128)(2,1)} %all-gather.13.cloned.1.call-done, f32[512,3072]{1,0:T(8,128)} %fusion.46, f32[3072]{0:T(1024)S(1)} %convert_element_type.173), kind=kOutput, calls=%fused_computation.132 | convolution fusion | flops 2432433664 | bytes 12600320 | tf_op jit(solution)/shard_map/dot_general | solution.py:26
  407.2 3.4 multiply_reduce_fusion.3
  412.6 2.5 fusion.40
  415.1 59.7 %all-reduce.7 = (bf16[3072]{0:T(1024)(128)(2,1)S(1)}, bf16[768]{0:T(1024)(128)(2,1)S(1)}) all-reduce(f32[3072]{0:T(1024)S(1)} %get-tuple-element.128, f32[768]{0:T(1024)S(1)} %get-tuple-element.107), channel_id=7, replica_groups=mesh['seq'=2,'fsdp'=16] {'fsdp'}, use_global_device_ids=true, to_apply=%region_28.29.clone | all-reduce | flops 3840 | bytes 23040
  478.3 100.5 %reduce-scatter.17.cloned.1.call-done = f32[192,768]{1,0:T(8,128)} async-done(((f32[3072,768]{1,0:T(8,128)}), f32[192,768]{1,0:T(8,128)}) %reduce-scatter.17.cloned.1.call-update) | async-done | bytes 589840 | tf_op jit(solution)/shard_map/reduce_scatter | solution.py:230
  580.6 113.9 %reduce-scatter.15.cloned.1.call-done = f32[48,3072]{1,0:T(8,128)} async-done(((f32[768,3072]{1,0:T(8,128)}), f32[48,3072]{1,0:T(8,128)}) %reduce-scatter.15.cloned.1.call-update) | async-done | bytes 589840 | tf_op jit(solution)/shard_map/reduce_scatter | solution.py:229
  699.5 54.4 %reduce-scatter.21.cloned.1.call-done = f32[48,2]{1,0:T(8,128)} async-done(((f32[768,2]{1,0:T(8,128)}), f32[48,2]{1,0:T(8,128)}) %reduce-scatter.21.cloned.1.call-update) | async-done | bytes 400
  754.8 58.1 %reduce-scatter.19.cloned.1.call-done = f32[48,3]{1,0:T(8,128)} async-done(((f32[768,3]{1,0:T(8,128)}), f32[48,3]{1,0:T(8,128)}) %reduce-scatter.19.cloned.1.call-update) | async-done | bytes 592
  813.7 4.9 all-reduce.9
  820.9 31.2 %all-reduce.13.cloned.1.call-done = (bf16[48,2304]{1,0:T(8,128)(2,1)}, bf16[48,768]{1,0:T(8,128)(2,1)}, bf16[48,3072]{1,0:T(8,128)(2,1)}, bf16[192,768]{1,0:T(8,128)(2,1)}) async-done(((bf16[48,2304]{1,0:T(8,128)(2,1)}, bf16[48,768]{1,0:T(8,128)(2,1)}, bf16[48,3072]{1,0:T(8,128)(2,1)}, bf16[192,768]{1,0:T(8,128)(2,1)}), (bf16[48,2304]{1,0:T(8,128)(2,1)}, bf16[48,768]{1,0:T(8,128)(2,1)}, ...) | async-done | bytes 884752 | tf_op jit(solution)/shard_map/psum | solution.py:239
  (219 shorter events, 75.4 us)
Async XLA Ops:
  7.2 5.4 copy-start.35
  7.2 28.5 %copy-start.34 = (bf16[3,48]{1,0:T(4,128)(2,1)S(1)}, bf16[3,48]{1,0:T(4,128)(2,1)}, u32[]{:S(2)}) copy-start(bf16[3,48]{1,0:T(4,128)(2,1)} %param.28) | copy-start | bytes 868
  7.2 53.1 %all-gather.7.cloned.1.call-start = ((), (), s32[]{:S(2)}) async-start(), calls=%async_computation.10 | async-start | bytes 3760128 | tf_op jit(solution)/shard_map/all_gather | solution.py:136
  7.9 176.1 %all-gather.9.cloned.1.call-start = ((), (), s32[]{:S(2)}) async-start(), calls=%async_computation.11 | async-start | bytes 1253376 | tf_op jit(solution)/shard_map/all_gather | solution.py:137
  8.7 178.3 %all-gather.11.cloned.1.call-start = ((), (), s32[]{:S(2)}) async-start(), calls=%async_computation.12 | async-start | bytes 5013504 | tf_op jit(solution)/shard_map/all_gather | solution.py:165
  9.4 199.4 %all-gather.13.cloned.1.call-start = ((), (), s32[]{:S(2)}) async-start(), calls=%async_computation.13 | async-start | bytes 5013504 | tf_op jit(solution)/shard_map/all_gather | solution.py:166
  12.6 173.9 %copy-start.2 = (f32[512,767]{1,0:T(8,128)}, f32[512,767]{1,0:T(8,128)S(1)}, u32[]{:S(2)}) copy-start(f32[512,767]{1,0:T(8,128)S(1)} %convert_bitcast_fusion) | copy-start | bytes 4712452
  54.0 11.8 %copy-start.31 = (f32[512]{0:T(512)}, f32[512]{0:T(512)S(1)}, u32[]{:S(2)}) copy-start(f32[512]{0:T(512)S(1)} %multiply_reduce_fusion.7) | copy-start | bytes 6148
  74.8 33.8 %all-to-all-start = ((bf16[512,3,2,384]{3,0,1,2:T(8,128)(2,1)}), bf16[512,3,2,384]{3,0,1,2:T(8,128)(2,1)}, u32[]{:S(2)}, u32[]{:S(2)}) async-start(bf16[512,3,2,384]{3,0,1,2:T(8,128)(2,1)} %copy.92), calls=%async_computation | async-start | bytes 4718592 | tf_op jit(solution)/shard_map/all_to_all | solution.py:146
  113.4 12.7 %copy-start.12 = (bf16[1024,1,1,384]{0,3,2,1:T(8,128)(2,1)}, bf16[1024,1,1,384]{0,3,2,1:T(8,128)(2,1)S(1)}, u32[]{:S(2)}) copy-start(bf16[1024,1,1,384]{0,3,2,1:T(8,128)(2,1)S(1)} %copy.100) | copy-start | bytes 2359300
  117.2 8.9 %copy-start.16 = (bf16[512,1,1,384]{0,3,2,1:T(8,128)(2,1)}, bf16[512,1,1,384]{0,3,2,1:T(8,128)(2,1)S(1)}, u32[]{:S(2)}) copy-start(bf16[512,1,1,384]{0,3,2,1:T(8,128)(2,1)S(1)} %copy.99) | copy-start | bytes 1179652
  118.5 6.7 copy-start.17
  125.2 6.7 copy-start.1
  137.5 7.0 copy-start.33
  137.5 8.9 %copy-start.38 = (bf16[48]{0:T(256)(128)(2,1)S(1)}, bf16[48]{0:T(256)(128)(2,1)}, u32[]{:S(2)}) copy-start(bf16[48]{0:T(256)(128)(2,1)} %param.30) | copy-start | bytes 292
  137.5 9.2 %copy-start.39 = (bf16[192]{0:T(256)(128)(2,1)S(1)}, bf16[192]{0:T(256)(128)(2,1)}, u32[]{:S(2)}) copy-start(bf16[192]{0:T(256)(128)(2,1)} %param.29) | copy-start | bytes 1156
  139.2 40.2 %copy-start.23 = (bf16[1,512,767]{2,1,0:T(8,128)(2,1)S(1)}, bf16[1,512,767]{2,1,0:T(8,128)(2,1)}, u32[]{:S(2)}) copy-start(bf16[1,512,767]{2,1,0:T(8,128)(2,1)} %param.23) | copy-start | bytes 2356228
  140.2 39.4 %all-to-all-start.1 = ((bf16[2,2,98304]{2,1,0:T(2,128)(2,1)}), bf16[2,2,98304]{2,1,0:T(2,128)(2,1)}, u32[]{:S(2)}, u32[]{:S(2)}) async-start(bf16[2,2,98304]{2,1,0:T(2,128)(2,1)} %reshape.344), calls=%async_computation.1 | async-start | bytes 1572864 | tf_op jit(solution)/shard_map/all_to_all | solution.py:158
  187.0 34.1 %copy-start.4 = (f32[512,768]{1,0:T(8,128)}, f32[512,768]{1,0:T(8,128)S(1)}, u32[]{:S(2)}) copy-start(f32[512,768]{1,0:T(8,128)S(1)} %get-tuple-element.100) | copy-start | bytes 4718596
  187.0 21.8 %copy-start.24 = (bf16[1,512,767]{2,1,0:T(8,128)(2,1)S(1)}, bf16[1,512,767]{2,1,0:T(8,128)(2,1)}, u32[]{:S(2)}) copy-start(bf16[1,512,767]{2,1,0:T(8,128)(2,1)} %param.23) | copy-start | bytes 2356228
  187.0 31.1 %slice-start.5 = ((s8[4718592]{0:T(1024)(128)(4,1)}), s8[524288]{0:T(1024)(128)(4,1)S(1)}, s32[]{:S(2)}) async-start(s8[4718592]{0:T(1024)(128)(4,1)} %bitcast.133), calls=%async_computation.26 | async-start | bytes 1048576
  208.8 9.3 %slice-start.6 = ((s8[4718592]{0:T(1024)(128)(4,1)}), s8[4194304]{0:T(1024)(128)(4,1)S(1)}, s32[]{:S(2)}) async-start(s8[4718592]{0:T(1024)(128)(4,1)} %bitcast.133), calls=%async_computation.27 | async-start | bytes 8388608
  222.3 5.4 copy-start.27
  224.1 15.0 %all-to-all-start.2 = ((bf16[512,2,384]{2,0,1:T(8,128)(2,1)}), bf16[512,2,384]{2,0,1:T(8,128)(2,1)S(1)}, u32[]{:S(2)}, u32[]{:S(2)}) async-start(bf16[512,2,384]{2,0,1:T(8,128)(2,1)} %bitcast.120), calls=%async_computation.2 | async-start | bytes 1572864 | tf_op jit(solution)/shard_map/all_to_all | solution.py:202
  227.6 247.3 %reduce-scatter.13.cloned.1.call-start = ((), (), s32[]{:S(2)}) async-start(), calls=%async_computation.15 | async-start | bytes 2506752 | tf_op jit(solution)/shard_map/reduce_scatter | solution.py:228
  229.9 246.6 %reduce-scatter.11.cloned.1.call-start = ((), (), s32[]{:S(2)}) async-start(), calls=%async_computation.14 | async-start | bytes 7520256 | tf_op jit(solution)/shard_map/reduce_scatter | solution.py:227
  240.1 5.0 copy-start.30
  245.1 26.0 %slice-start.3 = ((s8[6291456]{0:T(1024)(128)(4,1)}), s8[2097152]{0:T(1024)(128)(4,1)S(1)}, s32[]{:S(2)}) async-start(s8[6291456]{0:T(1024)(128)(4,1)} %bitcast.123), calls=%async_computation.24 | async-start | bytes 4194304
  254.0 10.1 %copy-start.19 = (bf16[1,512,1,384]{1,3,2,0:T(8,128)(2,1)S(1)}, bf16[1,512,1,384]{1,3,2,0:T(8,128)(2,1)}, u32[]{:S(2)}) copy-start(bf16[1,512,1,384]{1,3,2,0:T(8,128)(2,1)} %copy.106) | copy-start | bytes 1179652
  254.1 10.1 %copy-start.21 = (f32[512,6,64]{0,2,1:T(8,128)S(1)}, f32[512,6,64]{0,2,1:T(8,128)}, u32[]{:S(2)}) copy-start(f32[512,6,64]{0,2,1:T(8,128)} %fusion.28) | copy-start | bytes 2359300
  254.1 17.1 %slice-start.4 = ((s8[6291456]{0:T(1024)(128)(4,1)}), s8[4194304]{0:T(1024)(128)(4,1)S(1)}, s32[]{:S(2)}) async-start(s8[6291456]{0:T(1024)(128)(4,1)} %bitcast.123), calls=%async_computation.25 | async-start | bytes 8388608
  264.1 13.5 %slice-start = ((s8[12582912]{0:T(1024)(128)(4,1)}), s8[4194304]{0:T(1024)(128)(4,1)S(1)}, s32[]{:S(2)}) async-start(s8[12582912]{0:T(1024)(128)(4,1)} %bitcast.121), calls=%async_computation.21 | async-start | bytes 8388608
  264.1 13.4 %slice-start.1 = ((s8[12582912]{0:T(1024)(128)(4,1)}), s8[4194304]{0:T(1024)(128)(4,1)S(1)}, s32[]{:S(2)}) async-start(s8[12582912]{0:T(1024)(128)(4,1)} %bitcast.121), calls=%async_computation.22 | async-start | bytes 8388608
  271.2 6.4 slice-start.2
  277.6 9.6 %copy-start.6 = (bf16[6,512,512]{1,2,0:T(8,128)(2,1)S(1)}, bf16[6,512,512]{1,2,0:T(8,128)(2,1)}, u32[]{:S(2)}) copy-start(bf16[6,512,512]{1,2,0:T(8,128)(2,1)} %multiply_convert_fusion.1) | copy-start | bytes 9437188
  277.6 9.6 %copy-start.18 = (bf16[512,1,1,384]{0,3,2,1:T(8,128)(2,1)S(1)}, bf16[512,1,1,384]{0,3,2,1:T(8,128)(2,1)}, u32[]{:S(2)}) copy-start(bf16[512,1,1,384]{0,3,2,1:T(8,128)(2,1)} %copy-done.17) | copy-start | bytes 1179652
  310.5 6.1 copy-start.14
  310.5 6.1 copy-start.15
  375.0 203.8 %reduce-scatter.17.cloned.1.call-start = ((), (), s32[]{:S(2)}) async-start(), calls=%async_computation.17 | async-start | bytes 10027008 | tf_op jit(solution)/shard_map/reduce_scatter | solution.py:230
  386.9 307.7 %reduce-scatter.15.cloned.1.call-start = ((), (), s32[]{:S(2)}) async-start(), calls=%async_computation.16 | async-start | bytes 10027008 | tf_op jit(solution)/shard_map/reduce_scatter | solution.py:229
  395.8 358.2 %reduce-scatter.21.cloned.1.call-start = ((), (), s32[]{:S(2)}) async-start(), calls=%async_computation.19 | async-start | bytes 417792
  397.3 9.5 %copy-start.7 = (bf16[1024,3,1,384]{3,0,1,2:T(8,128)(2,1)S(1)}, bf16[1024,3,1,384]{3,0,1,2:T(8,128)(2,1)}, u32[]{:S(2)}) copy-start(bf16[1024,3,1,384]{3,0,1,2:T(8,128)(2,1)} %copy.112) | copy-start | bytes 7077892
  397.3 9.8 %copy-start.11 = (bf16[512,3,2,1,384]{0,4,2,1,3:T(8,128)(2,1)S(1)}, bf16[512,3,2,1,384]{0,4,2,1,3:T(8,128)(2,1)}, u32[]{:S(2)}) copy-start(bf16[512,3,2,1,384]{0,4,2,1,3:T(8,128)(2,1)} %copy.113) | copy-start | bytes 7077892
  397.4 9.8 %copy-start.36 = (bf16[768,2304]{1,0:T(8,128)(2,1)S(1)}, bf16[768,2304]{1,0:T(8,128)(2,1)}, u32[]{:S(2)}) copy-start(bf16[768,2304]{1,0:T(8,128)(2,1)} %all-gather.7.cloned.1.call-done) | copy-start | bytes 10616836
  411.5 401.4 %reduce-scatter.19.cloned.1.call-start = ((), (), s32[]{:S(2)}) async-start(), calls=%async_computation.18 | async-start | bytes 417792
  412.6 439.5 %all-reduce.13.cloned.1.call-start = ((), (), s32[]{:S(2)}) async-start(), calls=%async_computation.20 | async-start | bytes 1769472 | tf_op jit(solution)/shard_map/psum | solution.py:239
  412.6 283.8 %copy-start.32 = (f32[512]{0:T(512)S(1)}, f32[512]{0:T(512)}, u32[]{:S(2)}) copy-start(f32[512]{0:T(512)} %copy-done.31) | copy-start | bytes 6148
  415.1 281.3 %copy-start.9 = (f32[512,768]{1,0:T(8,128)S(1)}, f32[512,768]{1,0:T(8,128)}, u32[]{:S(2)}) copy-start(f32[512,768]{1,0:T(8,128)} %copy-done.8) | copy-start | bytes 4718596
  (13 other events, 29.6 us)
Sparse Core Ops, SparseCore 0:
  10.3 49.9 all-gather.6
  62.6 37.4 all-gather.8
  102.3 52.2 all-gather.10
  156.8 51.9 all-gather.12
  231.9 62.0 reduce-scatter.12
  375.1 88.5 reduce-scatter.10
  467.8 110.9 reduce-scatter.16
  583.4 111.0 reduce-scatter.14
  698.6 55.2 reduce-scatter.20
  758.3 54.5 reduce-scatter.18
  816.0 36.0 all-reduce.12
where the time goes:
time: 872 us; the launch traced here: 866 us
  waiting for transfers between devices  417 us (48%)
  blocking collectives  176 us (20%)
  matrix products  120 us (14%)
  local copies, waits for them, and re-layouts  63.4 us (7%)
  other arithmetic  57.3 us (7%)
  between operations  17.5 us (2%)
  starting transfers between devices  14.1 us (2%)
    unnamed x13, waiting for transfers between devices  115 us
    reduce_scatter x1, waiting for transfers between devices, local(): lax.psum_scatter(grad_fc, 'fsdp', scatter_dimension=0, tiled=True)  114 us
    reduce_scatter x1, waiting for transfers between devices, local(): lax.psum_scatter(grad_proj, 'fsdp', scatter_dimension=0, tiled=True)  100 us
    unnamed x2, blocking collectives  92.1 us
    all_to_all x1, blocking collectives, local(): lax.all_to_all(stacked, 'seq', split_axis=0, concat_axis=2, tiled=True)  38.6 us
    psum x1, waiting for transfers between devices, local(): lax.psum(shards[0].astype(jnp.bfloat16), 'seq').astype(jnp.float32)  31.2 us
    dot_general x4, matrix products, weight_grad(): lax.dot_general(inputs, grads, (((0,), (0,)), ((), ())), preferred_elemen...  27.1 us
    all_to_all x1, waiting for transfers between devices, local(): lax.all_to_all(projected.reshape(tok_rows, 3, seq_count, share), 'seq', s...  26.4 us
  transfers between devices with their start and end apart: 14, of which 9 were waited for; matrix products, arithmetic and copies ran while one was open for 25% of the time, Pallas kernels for 0%

commit v1 on v0

--- a/solution.py
+++ b/solution.py
@@ -1,13 +1,427 @@
+import functools
+
 import jax
 import jax.numpy as jnp
 from jax import lax
+from jax.experimental import pallas as pl
+from jax.experimental.pallas import tpu as pltpu
 from jax.sharding import PartitionSpec as P
 
 HD = 64
-
-
 EPSILON = 1e-05
 MASKED = -1e30
+MESH = pl.DeviceIdType.MESH
+ANY = pl.BlockSpec(memory_space=pl.ANY)
+
+
+class Place:
+    def __init__(self, shards):
+        self.length = shards // 4
+        self.x = lax.axis_index("seq")
+        index = lax.axis_index("fsdp")
+        self.index = index
+        self.core = lax.rem(index, 2)
+        self.y = lax.rem(index // 2, 2)
+        self.line = index // 4
+
+    def at(self, **moved):
+        x = moved.get("x", self.x)
+        line = moved.get("line", self.line)
+        y = moved.get("y", self.y)
+        core = moved.get("core", self.core)
+        return (x, (line * 2 + y) * 2 + core)
+
+    def beside_x(self):
+        return self.at(x=1 - self.x)
+
+    def beside_y(self):
+        return self.at(y=1 - self.y)
+
+    def sibling(self):
+        return self.at(core=1 - self.core)
+
+    def above(self):
+        return self.at(line=self.line + 1)
+
+    def below(self):
+        return self.at(line=self.line - 1)
+
+    def greet(self):
+        barrier = pltpu.get_barrier_semaphore()
+
+        def signal(device):
+            pl.semaphore_signal(barrier, inc=1, device_id=device, device_id_type=MESH)
+
+        signal(self.beside_x())
+        signal(self.beside_y())
+        signal(self.sibling())
+        has_below = self.line > 0
+        has_above = self.line < self.length - 1
+        pl.when(has_below)(lambda: signal(self.below()))
+        pl.when(has_above)(lambda: signal(self.above()))
+        pl.semaphore_wait(
+            barrier, 3 + has_below.astype(jnp.int32) + has_above.astype(jnp.int32)
+        )
+
+
+def remote(src, dst, send, recv, device):
+    return pltpu.make_async_remote_copy(
+        src_ref=src, dst_ref=dst, send_sem=send, recv_sem=recv, device_id=device, device_id_type=MESH
+    )
+
+
+class Gather:
+    def __init__(self, place, shard, out, sems):
+        self.p = place
+        self.shard = shard
+        self.out = out
+        self.rows, self.cols = shard.shape
+        (self.up, self.down, self.line_in, self.ys, self.yr, self.xs, self.xr, self.ds, self.dr, self.own) = sems
+
+    @staticmethod
+    def sem_shapes(length):
+        dma = pltpu.SemaphoreType.DMA
+        return [dma((length,))] * 7 + [dma((3, length))] * 2 + [dma]
+
+    def half(self, ref, which):
+        width = self.cols // 2
+        return ref.at[:, pl.ds(pl.multiple_of(which * width, width), width)]
+
+    def slot(self, line, y, core):
+        return self.out.at[line, y, core]
+
+    def up_copy(self, line, src=None):
+        p = self.p
+        dst = self.slot(line, p.y, p.core)
+        return remote(dst if src is None else src, dst, self.up.at[line], self.line_in.at[line], p.above())
+
+    def down_copy(self, line, src=None):
+        p = self.p
+        dst = self.slot(line, p.y, p.core)
+        return remote(dst if src is None else src, dst, self.down.at[line], self.line_in.at[line], p.below())
+
+    def y_copy(self, line, src=None):
+        p = self.p
+        dst = self.half(self.slot(line, p.y, p.core), p.x)
+        src = dst if src is None else self.half(src, p.x)
+        return remote(src, dst, self.ys.at[line], self.yr.at[line], p.beside_y())
+
+    def y_landing(self, line):
+        p = self.p
+        dst = self.half(self.slot(line, 1 - p.y, p.core), p.x)
+        return remote(dst, dst, self.ys.at[line], self.yr.at[line], p.beside_y())
+
+    def x_copy(self, line):
+        p = self.p
+        dst = self.half(self.slot(line, 1 - p.y, p.core), p.x)
+        return remote(dst, dst, self.xs.at[line], self.xr.at[line], p.beside_x())
+
+    def x_landing(self, line):
+        p = self.p
+        dst = self.half(self.slot(line, 1 - p.y, p.core), 1 - p.x)
+        return remote(dst, dst, self.xs.at[line], self.xr.at[line], p.beside_x())
+
+    def d_copy(self, kind, line, src=None, core=None):
+        p = self.p
+        core = p.core if core is None else core
+        if kind == 0:
+            dst = self.slot(line, p.y, core)
+        else:
+            dst = self.half(self.slot(line, 1 - p.y, core), p.x if kind == 1 else 1 - p.x)
+        return remote(dst if src is None else src, dst, self.ds.at[kind, line], self.dr.at[kind, line], p.sibling())
+
+    def own_copy(self):
+        p = self.p
+        return pltpu.make_async_copy(self.shard, self.slot(p.line, p.y, p.core), self.own)
+
+    def each_at(self, distance, act):
+        p = self.p
+        if distance == 0:
+            act(p.line, 0)
+            return
+        pl.when(p.line - distance >= 0)(lambda: act(p.line - distance, 1))
+        pl.when(p.line + distance < p.length)(lambda: act(p.line + distance, -1))
+
+    def arrive(self, distance):
+        p = self.p
+
+        def act(line, way):
+            src = None
+            if way == 0:
+                src = self.shard
+                self.own_copy().start()
+            else:
+                self.up_copy(line).wait_recv()
+            if way >= 0:
+                pl.when(p.line < p.length - 1)(lambda: self.up_copy(line, src).start())
+            if way <= 0:
+                pl.when(p.line > 0)(lambda: self.down_copy(line, src).start())
+            self.y_copy(line, src).start()
+            self.d_copy(0, line, src).start()
+
+        self.each_at(distance, act)
+
+    def arrive_y(self, distance):
+        def act(line, way):
+            self.y_landing(line).wait_recv()
+            self.x_copy(line).start()
+            self.d_copy(1, line).start()
+
+        self.each_at(distance, act)
+
+    def arrive_x(self, distance):
+        def act(line, way):
+            self.x_landing(line).wait_recv()
+            self.d_copy(2, line).start()
+
+        self.each_at(distance, act)
+
+    def stage(self, time):
+        length = self.p.length
+        if 0 <= time < length:
+            self.arrive(time)
+        if 0 <= time - 1 < length:
+            self.arrive_y(time - 1)
+        if 0 <= time - 2 < length:
+            self.arrive_x(time - 2)
+
+    def stages(self):
+        return self.p.length + 2
+
+    def finish(self):
+        p = self.p
+
+        def one(line):
+            for kind in range(3):
+                self.d_copy(kind, line, core=1 - p.core).wait_recv()
+            for kind in range(3):
+                self.d_copy(kind, line).wait_send()
+            self.y_copy(line).wait_send()
+            self.x_copy(line).wait_send()
+            pl.when((p.line >= line) & (p.line < p.length - 1))(lambda: self.up_copy(line).wait_send())
+            pl.when((p.line <= line) & (p.line > 0))(lambda: self.down_copy(line).wait_send())
+
+        for line in range(p.length):
+            one(line)
+        self.own_copy().wait()
+
+
+def gather_kernel(shards, lag, count, *refs):
+    ins, outs, rest = refs[:count], refs[count : 2 * count], refs[2 * count :]
+    place = Place(shards)
+    place.greet()
+    per = len(Gather.sem_shapes(1))
+    gathers = [Gather(place, ins[k], outs[k], rest[k * per : (k + 1) * per]) for k in range(count)]
+    total = max(lag[k] + g.stages() for k, g in enumerate(gathers))
+    for time in range(total):
+        for k, g in enumerate(gathers):
+            g.stage(time - lag[k])
+    for g in gathers:
+        g.finish()
+
+
+def gather_all(arrays, shards, lag, collective_id):
+    length = shards // 4
+    out = pl.pallas_call(
+        functools.partial(gather_kernel, shards, lag, len(arrays)),
+        out_shape=[jax.ShapeDtypeStruct((length, 2, 2) + a.shape, a.dtype) for a in arrays],
+        in_specs=[ANY] * len(arrays),
+        out_specs=[ANY] * len(arrays),
+        scratch_shapes=Gather.sem_shapes(length) * len(arrays),
+        compiler_params=pltpu.CompilerParams(collective_id=collective_id, has_side_effects=True),
+        name="gather_weights",
+    )(*arrays)
+    return [o.reshape((shards,) + a.shape) for o, a in zip(out, arrays)]
+
+
+class Scatter:
+    def __init__(self, place, partial, out, refs):
+        self.p = place
+        self.g = partial
+        self.out = out
+        self.rows, self.cols = out.shape
+        (self.s, self.d, self.xb, self.yb, self.lo, self.hi, self.fb, self.tb,
+         self.load, self.ds, self.dr, self.xs, self.xr, self.ys, self.yr,
+         self.us, self.ur, self.ns, self.nr, self.fs, self.fr) = refs
+
+    @staticmethod
+    def scratch(length, rows, cols, dtype):
+        dma = pltpu.SemaphoreType.DMA
+        full = pltpu.VMEM((length, 2, rows, cols), dtype)
+        half = pltpu.VMEM((length, rows, cols // 2), dtype)
+        line = pltpu.VMEM((length, rows, cols), dtype)
+        one = pltpu.VMEM((rows, cols), dtype)
+        return [full, full, half, half, line, line, one, one] + [dma] * 7 + [dma((length,))] * 4 + [dma] * 2
+
+    def half(self, which):
+        width = self.cols // 2
+        return pl.ds(pl.multiple_of(which * width, width), width)
+
+    def load_copy(self):
+        return pltpu.make_async_copy(self.g.at[:, :, self.p.core], self.s, self.load)
+
+    def d_copy(self):
+        p = self.p
+        return remote(self.g.at[:, :, 1 - p.core], self.d, self.ds, self.dr, p.sibling())
+
+    def x_copy(self):
+        p = self.p
+        src = self.s.at[:, 1 - p.y, :, self.half(1 - p.x)]
+        return remote(src, self.xb, self.xs, self.xr, p.beside_x())
+
+    def y_copy(self):
+        p = self.p
+        src = self.s.at[:, 1 - p.y, :, self.half(p.x)]
+        return remote(src, self.yb, self.ys, self.yr, p.beside_y())
+
+    def up_copy(self, line):
+        p = self.p
+        return remote(self.s.at[line, p.y], self.lo.at[line], self.us.at[line], self.ur.at[line], p.above())
+
+    def down_copy(self, line):
+        p = self.p
+        return remote(self.s.at[line, p.y], self.hi.at[line], self.ns.at[line], self.nr.at[line], p.below())
+
+    def f_copy(self):
+        return remote(self.tb, self.fb, self.fs, self.fr, self.p.beside_x())
+
+    def each(self, act):
+        def body(line, carry):
+            act(line)
+            return carry
+
+        lax.fori_loop(0, self.p.length, body, 0)
+
+    def start(self):
+        self.load_copy().start()
+        self.d_copy().start()
+
+    def pair(self):
+        p = self.p
+        self.load_copy().wait()
+        self.d_copy().wait()
+
+        def other(line):
+            self.s[line, 1 - p.y] = self.s[line, 1 - p.y] + self.d[line, 1 - p.y]
+
+        self.each(other)
+        self.x_copy().start()
+
+        def own(line):
+            self.s[line, p.y] = self.s[line, p.y] + self.d[line, p.y]
+
+        self.each(own)
+
+    def over_x(self):
+        p = self.p
+        self.x_copy().wait()
+
+        def act(line):
+            cols = self.half(p.x)
+            self.s[line, 1 - p.y, :, cols] = self.s[line, 1 - p.y, :, cols] + self.xb[line]
+
+        self.each(act)
+        self.y_copy().start()
+
+    def over_y(self):
+        p = self.p
+        self.y_copy().wait()
+
+        def act(line):
+            cols = self.half(p.x)
+            self.s[line, p.y, :, cols] = self.s[line, p.y, :, cols] + self.yb[line]
+
+        self.each(act)
+
+    def hop(self, step):
+        p = self.p
+        last = p.length - 1
+        up = last - step + p.line
+
+        def upward():
+            @pl.when(p.line > 0)
+            def _():
+                self.up_copy(up).wait_recv()
+                self.s[up, p.y] = self.s[up, p.y] + self.lo[up]
+
+            self.up_copy(up).start()
+
+        pl.when(p.line <= step)(upward)
+        down = step - last + p.line
+
+        def downward():
+            @pl.when(p.line < last)
+            def _():
+                self.down_copy(down).wait_recv()
+                self.s[down, p.y] = self.s[down, p.y] + self.hi[down]
+
+            self.down_copy(down).start()
+
+        pl.when(down >= 0)(downward)
+
+    def total(self):
+        p = self.p
+        mine = p.line
+
+        @pl.when(p.line > 0)
+        def _():
+            self.up_copy(mine).wait_recv()
+            self.s[mine, p.y] = self.s[mine, p.y] + self.lo[mine]
+
+        @pl.when(p.line < p.length - 1)
+        def _():
+            self.down_copy(mine).wait_recv()
+            self.s[mine, p.y] = self.s[mine, p.y] + self.hi[mine]
+
+        self.tb[...] = self.s[mine, p.y]
+        self.f_copy().start()
+
+    def finish(self):
+        p = self.p
+        self.f_copy().wait()
+        self.out[...] = self.tb[...].astype(jnp.float32) + self.fb[...].astype(jnp.float32)
+        for line in range(p.length):
+            pl.when(line > p.line)(lambda line=line: self.up_copy(line).wait_send())
+            pl.when(line < p.line)(lambda line=line: self.down_copy(line).wait_send())
+
+    def stages(self):
+        acts = [self.start, self.pair, self.over_x, self.over_y]
+        acts += [functools.partial(self.hop, step) for step in range(self.p.length - 1)]
+        return acts + [self.total, self.finish]
+
+
+def scatter_kernel(shards, lag, count, *refs):
+    ins, outs, rest = refs[:count], refs[count : 2 * count], refs[2 * count :]
+    place = Place(shards)
+    place.greet()
+    per = len(rest) // count
+    lists = [
+        Scatter(place, ins[k], outs[k], rest[k * per : (k + 1) * per]).stages() for k in range(count)
+    ]
+    total = max(lag[k] + len(s) for k, s in enumerate(lists))
+    for time in range(total):
+        for k, acts in enumerate(lists):
+            if 0 <= time - lag[k] < len(acts):
+                acts[time - lag[k]]()
+
+
+def scatter_all(arrays, shards, lag, collective_id):
+    length = shards // 4
+    parts = [a.reshape((length, 2, 2) + a.shape[1:]) for a in arrays]
+    scratch = []
+    for a in arrays:
+        scratch += Scatter.scratch(length, a.shape[1], a.shape[2], a.dtype)
+    return pl.pallas_call(
+        functools.partial(scatter_kernel, shards, lag, len(arrays)),
+        out_shape=[jax.ShapeDtypeStruct(a.shape[1:], jnp.float32) for a in arrays],
+        in_specs=[ANY] * len(arrays),
+        out_specs=[pl.BlockSpec(memory_space=pltpu.VMEM)] * len(arrays),
+        scratch_shapes=scratch,
+        compiler_params=pltpu.CompilerParams(
+            collective_id=collective_id, has_side_effects=True, vmem_limit_bytes=60 << 20
+        ),
+        name="scatter_grads",
+    )(*parts)
 
 
 def rms_norm(values, gain):
@@ -123,65 +537,77 @@
     )
 
 
+def swap_halves(value):
+    shards = lax.axis_size("fsdp")
+    pairs = []
+    for x in range(2):
+        for index in range(shards):
+            core = index % 2
+            goal = (x, index) if core == x else (1 - x, index ^ 1)
+            pairs.append((x * shards + index, goal[0] * shards + goal[1]))
+    return lax.ppermute(value, ("seq", "fsdp"), pairs)
+
+
+def pair_all_to_all(value, split_axis, concat_axis):
+    shards = lax.axis_size("fsdp")
+    groups = [[k, k + 1] for k in range(0, shards, 2)]
+    return lax.all_to_all(
+        value, "fsdp", split_axis=split_axis, concat_axis=concat_axis, axis_index_groups=groups, tiled=True
+    )
+
+
+def column_parts(cols):
+    return 3 if cols % 768 == 0 and cols >= 2304 else 1
+
+
+def pack_rows(parts, width):
+    rows = [jnp.pad(p, ((0, 0), (0, width - p.shape[1]))) for p in parts]
+    packed = jnp.concatenate(rows, axis=0)
+    return jnp.pad(packed, ((0, 16 - packed.shape[0]), (0, 0)))
+
+
 def local(residual_in, cotangent, w_qkv, w_out, w_fc, w_proj, attn_bias, fc_bias, proj_bias, gains):
-    seq_count = lax.axis_size("seq")
+    shards = lax.axis_size("fsdp")
     tok_rows = residual_in.shape[1]
     model_width = w_qkv.shape[1] // 3
-    share = model_width // seq_count
+    hidden_width = w_fc.shape[1]
+    unit = gains.shape[1]
+    share = model_width // 2
     head_count = share // HD
     scale = HD ** (-0.5)
-    compact = residual_in[0].astype(jnp.float32)
+    small = pack_rows([attn_bias, gains, proj_bias[None], fc_bias[None]], 256)
+    compact = swap_halves(residual_in[0]).astype(jnp.float32)
+    upstream = swap_halves(cotangent[0]).astype(jnp.float32)
+    qkv_w, small_all, out_w, fc_w, proj_w = gather_all(
+        [w_qkv, small, w_out, w_fc, w_proj], shards, [0, 0, 2, 3, 5], 0
+    )
+    qkv_w = qkv_w.reshape(model_width, 3 * model_width)
+    out_w = out_w.reshape(model_width, model_width)
+    fc_w = fc_w.reshape(model_width, hidden_width)
+    proj_w = proj_w.reshape(hidden_width, model_width)
+    vectors = small_all[:, :6, :unit].transpose(1, 0, 2).reshape(6, model_width).astype(jnp.float32)
+    bias_all, gain_all, proj_b = vectors[:3], vectors[3:5], vectors[5]
+    fc_b = small_all[:, 6, : fc_bias.shape[0]].reshape(hidden_width).astype(jnp.float32)
     full = jnp.concatenate([compact, -jnp.sum(compact, axis=-1, keepdims=True)], axis=-1)
-    qkv_w, out_w, attn_b, gain_w = (
-        lax.all_gather(w_qkv, "fsdp", axis=0, tiled=True),
-        lax.all_gather(w_out, "fsdp", axis=0, tiled=True),
-        lax.all_gather(attn_bias, "fsdp", axis=1, tiled=True),
-        lax.all_gather(gains, "fsdp", axis=1, tiled=True),
-    )
-    gain_all = gain_w.astype(jnp.float32)
-    bias_all = attn_b.astype(jnp.float32)
     normed = rms_norm(full, gain_all[0]).astype(jnp.bfloat16)
     bias_qkv = jnp.concatenate([bias_all[0], jnp.zeros_like(bias_all[0]), bias_all[1]])
     projected = (matmul(normed, qkv_w) + bias_qkv).astype(jnp.bfloat16)
-    by_heads = lax.all_to_all(
-        projected.reshape(tok_rows, 3, seq_count, share),
-        "seq",
-        split_axis=2,
-        concat_axis=0,
-        tiled=True,
-    )
+    by_heads = pair_all_to_all(projected.reshape(tok_rows, 3, 2, share), 2, 0)
     length = by_heads.shape[0]
     queries = by_heads[:, 0, 0].reshape(length, head_count, HD)
     keys_all = by_heads[:, 1, 0].reshape(length, head_count, HD)
     values_all = by_heads[:, 2, 0].reshape(length, head_count, HD)
     attended, log_totals = attend(queries, keys_all, values_all, scale)
-    mixed = lax.all_to_all(
-        attended.reshape(length, 1, share), "seq", split_axis=0, concat_axis=1, tiled=True
-    )
+    mixed = pair_all_to_all(attended.reshape(length, 1, share), 0, 1)
     mixed = mixed.reshape(tok_rows, model_width)
     branch = matmul(mixed, out_w) + bias_all[2]
     middle = full + center(branch)
-    fc_w, proj_w, fc_b, proj_b = (
-        lax.all_gather(w_fc, "fsdp", axis=0, tiled=True),
-        lax.all_gather(w_proj, "fsdp", axis=0, tiled=True),
-        lax.all_gather(fc_bias, "fsdp", axis=0, tiled=True),
-        lax.all_gather(proj_bias, "fsdp", axis=0, tiled=True),
-    )
     normed_two = rms_norm(middle, gain_all[1]).astype(jnp.bfloat16)
-    hidden = matmul(normed_two, fc_w) + fc_b.astype(jnp.float32)
+    hidden = matmul(normed_two, fc_w) + fc_b
     activated = gelu_tanh(hidden).astype(jnp.bfloat16)
-    branch_two = matmul(activated, proj_w) + proj_b.astype(jnp.float32)
+    branch_two = matmul(activated, proj_w) + proj_b
     final = middle + center(branch_two)
-    residual_out = final[:, :-1].astype(jnp.bfloat16)[None]
-    qkv_w, out_w, fc_w, proj_w, gain_w = (
-        lax.all_gather(w_qkv, "fsdp", axis=0, tiled=True),
-        lax.all_gather(w_out, "fsdp", axis=0, tiled=True),
-        lax.all_gather(w_fc, "fsdp", axis=0, tiled=True),
-        lax.all_gather(w_proj, "fsdp", axis=0, tiled=True),
-        lax.all_gather(gains, "fsdp", axis=1, tiled=True),
-    )
-    gain_all = gain_w.astype(jnp.float32)
-    upstream = cotangent[0].astype(jnp.float32)
+    residual_out = swap_halves(final[:, :-1].astype(jnp.bfloat16))[None]
     grad_final = jnp.concatenate([upstream, jnp.zeros((tok_rows, 1), jnp.float32)], axis=-1)
     grad_branch_two = center(grad_final).astype(jnp.bfloat16)
     grad_proj = weight_grad(activated, grad_branch_two)
@@ -199,63 +625,61 @@
     grad_out = weight_grad(mixed, grad_branch)
     grad_out_bias = jnp.sum(grad_branch.astype(jnp.float32), axis=0)
     grad_mixed = input_grad_of(grad_branch, out_w).astype(jnp.bfloat16)
-    grad_heads = lax.all_to_all(
-        grad_mixed.reshape(tok_rows, seq_count, share),
-        "seq",
-        split_axis=1,
-        concat_axis=0,
-        tiled=True,
-    )
+    grad_heads = pair_all_to_all(grad_mixed.reshape(tok_rows, 2, share), 1, 0)
     grad_heads = grad_heads.reshape(length, head_count, HD)
     grad_queries, grad_keys, grad_values = attend_back(
         queries, keys_all, values_all, log_totals, grad_heads, scale
     )
     stacked = jnp.stack([grad_queries, grad_keys, grad_values], axis=1).reshape(length, 3, 1, share)
-    grad_projected = lax.all_to_all(stacked, "seq", split_axis=0, concat_axis=2, tiled=True)
+    grad_projected = pair_all_to_all(stacked, 0, 2)
     grad_projected = grad_projected.reshape(tok_rows, 3 * model_width)
     grad_qkv = weight_grad(normed, grad_projected)
     column_sums = jnp.sum(grad_projected.astype(jnp.float32), axis=0)
-    grad_attn_bias = jnp.stack(
-        [column_sums[:model_width], column_sums[2 * model_width :], grad_out_bias]
-    )
     grad_normed = input_grad_of(grad_projected, qkv_w)
     first_pull = jax.vjp(rms_norm, full, gain_all[0])[1]
     grad_full_norm, grad_gain_one = first_pull(grad_normed)
     grad_full = grad_middle + grad_full_norm
-    input_grad = (grad_full[:, :-1] - grad_full[:, -1:]).astype(jnp.bfloat16)[None]
-    shards = (
-        lax.psum_scatter(grad_qkv, "fsdp", scatter_dimension=0, tiled=True),
-        lax.psum_scatter(grad_out, "fsdp", scatter_dimension=0, tiled=True),
-        lax.psum_scatter(grad_fc, "fsdp", scatter_dimension=0, tiled=True),
-        lax.psum_scatter(grad_proj, "fsdp", scatter_dimension=0, tiled=True),
-        lax.psum_scatter(grad_attn_bias, "fsdp", scatter_dimension=1, tiled=True),
-        lax.psum_scatter(grad_fc_bias, "fsdp", scatter_dimension=0, tiled=True),
-        lax.psum_scatter(grad_proj_bias, "fsdp", scatter_dimension=0, tiled=True),
-        lax.psum_scatter(
-            jnp.stack([grad_gain_one, grad_gain_two]), "fsdp", scatter_dimension=1, tiled=True
-        ),
-    )
-    totals = (
-        lax.psum(shards[0].astype(jnp.bfloat16), "seq").astype(jnp.float32),
-        lax.psum(shards[1].astype(jnp.bfloat16), "seq").astype(jnp.float32),
-        lax.psum(shards[2].astype(jnp.bfloat16), "seq").astype(jnp.float32),
-        lax.psum(shards[3].astype(jnp.bfloat16), "seq").astype(jnp.float32),
-        lax.psum(shards[4].astype(jnp.bfloat16), "seq").astype(jnp.float32),
-        lax.psum(shards[5].astype(jnp.bfloat16), "seq").astype(jnp.float32),
-        lax.psum(shards[6].astype(jnp.bfloat16), "seq").astype(jnp.float32),
-        lax.psum(shards[7].astype(jnp.bfloat16), "seq").astype(jnp.float32),
+    input_grad = swap_halves((grad_full[:, :-1] - grad_full[:, -1:]).astype(jnp.bfloat16))[None]
+    rows = jnp.stack(
+        [
+            column_sums[:model_width],
+            column_sums[2 * model_width :],
+            grad_out_bias,
+            grad_gain_one,
+            grad_gain_two,
+            grad_proj_bias,
+        ]
+    )
+    rows = rows.reshape(6, shards, unit).transpose(1, 0, 2)
+    last = grad_fc_bias.reshape(shards, 1, fc_bias.shape[0])
+    grad_small = jnp.concatenate(
+        [
+            jnp.pad(rows, ((0, 0), (0, 0), (0, 256 - unit))),
+            jnp.pad(last, ((0, 0), (0, 9), (0, 256 - fc_bias.shape[0]))),
+        ],
+        axis=1,
+    )
+
+    def split(grad):
+        return grad.astype(jnp.bfloat16).reshape(shards, grad.shape[0] // shards, grad.shape[1])
+
+    total_proj, total_fc, total_out, total_qkv, total_small = scatter_all(
+        [split(grad_proj), split(grad_fc), split(grad_out), split(grad_qkv), grad_small.astype(jnp.bfloat16)],
+        shards,
+        [0, 1, 2, 3, 3],
+        1,
     )
     return (
         residual_out,
         input_grad,
-        totals[0],
-        totals[1],
-        totals[2],
-        totals[3],
-        totals[4],
-        totals[5],
-        totals[6],
-        totals[7],
+        total_qkv,
+        total_out,
+        total_fc,
+        total_proj,
+        total_small[:3, :unit],
+        total_small[6, : fc_bias.shape[0]],
+        total_small[5, :unit],
+        total_small[3:5, :unit],
     )
 
 

time: 872 us -> 458 us (0.53)
  waiting for transfers between devices: 417 us -> 0.01 us
  Pallas kernels: 0 us -> 195 us
  blocking collectives: 176 us -> 22.1 us
  matrix products: 120 us -> 97.6 us
  between operations: 17.5 us -> 2 us
  other arithmetic: 57.3 us -> 44 us
  local copies, waits for them, and re-layouts: 63.4 us -> 75.9 us
    reduce_scatter x4 -> x0, waiting for transfers between devices: 214 us -> none  [the longest x1 114 us: local(): lax.psum_scatter(grad_fc, 'fsdp', scatter_dimension=0, tiled=True)]
    pallas_call x0 -> x2, Pallas kernels: none -> 195 us  [the longest x1 109 us: scatter_all(): pl.pallas_call(functools.partial(scatter_kernel, shards, lag, len(arrays)...]
    unnamed x13 -> x0, waiting for transfers between devices: 115 us -> none
    unnamed x2 -> x0, blocking collectives: 92.1 us -> none
    all_gather x2 -> x0, blocking collectives: 40.7 us -> none  [the longest x1 23 us: local(): lax.all_gather(gains, 'fsdp', axis=1, tiled=True)]
    all_to_all x3 -> x0, waiting for transfers between devices: 35.4 us -> none  [the longest x1 26.4 us: local(): lax.all_to_all(projected.reshape(tok_rows, 3, seq_count, share), 'seq', s...]
    psum x1 -> x0, waiting for transfers between devices: 31.2 us -> none  [local(): lax.psum(shards[0].astype(jnp.bfloat16), 'seq').astype(jnp.float32)]
    all_gather x4 -> x0, waiting for transfers between devices: 20.5 us -> none  [the longest x1 14.2 us: local(): lax.all_gather(w_proj, 'fsdp', axis=0, tiled=True)]
  transfers between devices with their start and end apart: 14 -> 4, of which waited for: 9 -> 0; matrix products, arithmetic and copies ran while one was open for 25% -> 11% of each run, Pallas kernels for 0% -> 43%
where the time goes in v1:
time: 458 us; the launch traced here: 449 us
  Pallas kernels  195 us (43%)
  matrix products  97.6 us (21%)
  local copies, waits for them, and re-layouts  75.9 us (17%)
  other arithmetic  44 us (10%)
  blocking collectives  22.1 us (5%)
  starting transfers between devices  13 us (3%)
    pallas_call x1, Pallas kernels, scatter_all(): pl.pallas_call(functools.partial(scatter_kernel, shards, lag, len(arrays)...  109 us
    pallas_call x1, Pallas kernels, gather_all(): pl.pallas_call(functools.partial(gather_kernel, shards, lag, len(arrays))...  85.6 us
    all_to_all x4, blocking collectives, pair_all_to_all(): lax.all_to_all(value, 'fsdp', split_axis=split_axis, concat_axis=concat_a...  22.1 us
    dot_general x4, matrix products, input_grad_of(): lax.dot_general(grads, weight, (((1,), (1,)), ((), ())), preferred_elemen...  20 us
    dot_general x4, matrix products, weight_grad(): lax.dot_general(inputs, grads, (((0,), (0,)), ((), ())), preferred_elemen...  19.3 us
    another operation x3, local copies, waits for them, and re-layouts, local(): jnp.stack([grad_queries, grad_keys, grad_values], axis=1)  14.5 us
    dot_general x2, matrix products, attend_back(): jnp.einsum('qhd,khd->hqk', grad_block, values_all[:finish], preferred_ele...  14.3 us
    unnamed x150, local copies, waits for them, and re-layouts  13.9 us
  transfers between devices with their start and end apart: 4, of which 0 were waited for; matrix products, arithmetic and copies ran while one was open for 11% of the time, Pallas kernels for 43%

profile of v1, /device:TPU:0, one launch (start us, length us, event | category | flops | bytes accessed | tf_op | source)
XLA Modules:
  0.0 449.5 jit_solution(9665979315056097050)
XLA Ops:
  6.2 85.6 %gather_weights.1 = (bf16[4,2,2,48,2304]{4,3,2,1,0:T(8,128)(2,1)}, bf16[4,2,2,16,256]{4,3,2,1,0:T(8,128)(2,1)}, bf16[4,2,2,48,768]{4,3,2,1,0:T(8,128)(2,1)}, bf1...) custom-call(bf16[48,2304]{1,0:T(8,128)(2,1)} %refs_0_.1, bf16[16,256]{1,0:T(8,128)(2,1)} %pad.48.refs_1_, ...), custom_call_target="tpu_custom_call" | custom-call | tf_op jit(solution)/shard_map/gather_weights/pallas_call | solution.py:225
  101.0 3.5 fusion.15
  104.5 5.6 %reshape.354 = bf16[512,3,2,384]{3,2,1,0:T(2,128)(2,1)} reshape(bf16[512,2304]{1,0:T(8,128)(2,1)} %fusion.15) | data formatting | bytes 4718592 | tf_op jit(solution)/shard_map/reshape | solution.py:595
  110.0 2.0 copy.65
  112.0 5.8 %all_to_all.63 = bf16[512,3,2,384]{3,0,1,2:T(8,128)(2,1)S(1)} all-to-all(bf16[512,3,2,384]{3,0,1,2:T(8,128)(2,1)S(1)} %copy.65), channel_id=1, replica_groups={{0,1},{2,3},{4,5},{6,7},{8,9},{10,11},{12,13},{14,15},{16,17},{18,19},{..., dimensions={2} | all-to-all | bytes 4718592 | tf_op jit(solution)/shard_map/all_to_all | solution.py:554
  124.9 1.9 copy.68
  126.9 1.9 copy.67
  128.8 2.3 copy.71
  131.1 2.4 fusion.66
  137.4 2.4 fusion.65
  139.8 2.8 fusion
  144.3 3.3 fusion.38
  150.1 5.5 %all_to_all.64 = bf16[2,2,98304]{2,1,0:T(2,128)(2,1)} all-to-all(bf16[2,2,98304]{2,1,0:T(2,128)(2,1)S(1)} %reshape.395), channel_id=1, replica_groups={{0,1},{2,3},{4,5},{6,7},{8,9},{10,11},{12,13},{14,15},{16,17},{18,19},{..., dimensions={0} | all-to-all | bytes 1572864 | tf_op jit(solution)/shard_map/all_to_all | solution.py:554
  159.8 2.5 fusion.67
  163.1 2.7 fusion.52
  165.9 9.0 %fusion.69 = (bf16[3072]{0:T(1024)(128)(2,1)}, bf16[512,3072]{1,0:T(8,128)(2,1)S(1)}) fusion(f32[512,3072]{1,0:T(8,128)S(1)} %fusion.52, f32[3072]{0:T(1024)S(1)} %copy-done.41, bf16[3072,768]{1,0:T(8,128)(2,1)S(1)} %bitcast.166, f32[512]{0:T(512)S(1)} %copy-done.48, bf16[512,767]{1,0:T(8,128)(2,1)S(1)} %copy-done.5), kind=kOutput, calls=%fused_computation.148 | convolution fusion | flops 2451698688 | bytes 14961664 | tf_op jit(solution)/shard_map/dot_general | solution.py:450
  174.9 3.3 multiply_reduce_fusion.2
  180.8 1.8 convolution_convert_fusion.3
  182.6 4.5 %all_to_all.65 = bf16[512,2,384]{2,0,1:T(8,128)(2,1)S(1)} all-to-all(bf16[512,2,384]{2,0,1:T(8,128)(2,1)S(1)} %bitcast.144), channel_id=1, replica_groups={{0,1},{2,3},{4,5},{6,7},{8,9},{10,11},{12,13},{14,15},{16,17},{18,19},{..., dimensions={1} | all-to-all | bytes 1572864 | tf_op jit(solution)/shard_map/all_to_all | solution.py:554
  188.1 1.9 copy.77
  190.0 4.9 %fusion.28 = f32[512,6,64]{0,2,1:T(8,128)} fusion(bf16[512,6,64]{0,2,1:T(8,128)(2,1)} %bitcast.130, f32[6,512,512]{1,2,0:T(8,128)} %copy-done.1, f32[6,512]{1,0:T(8,128)} %log_add_fusion.1), kind=kOutput, calls=%fused_computation.70 | convolution fusion | flops 204472320 | bytes 7483392 | tf_op jit(solution)/shard_map/hqk,qhd->khd/dot_general | solution.py:524
  195.0 4.3 multiply_reduce_fusion.1
  199.4 1.9 multiply_convert_fusion.1
  201.3 2.4 fusion.36
  203.7 2.0 fusion.31
  205.6 1.9 copy.79
  207.6 9.9 %multiply_reduce_fusion = (f32[6,512]{1,0:T(8,128)}, f32[6,512,1024]{2,1,0:T(8,128)}) fusion(f32[6,512,1024]{2,1,0:T(8,128)} %copy-done, f32[6,512]{1,0:T(8,128)S(1)} %log_add_fusion, bf16[512,6,64]{0,2,1:T(8,128)(2,1)} %bitcast.137, bf16[1024,6,64]{0,2,1:T(8,128)(2,1)} %bitcast.139), kind=kOutput, calls=%fused_computation.1 | convolution fusion | flops 412087296 | bytes 26370048 | tf_op jit(solution)/shard_map/qhd,khd->hqk/dot_general | solution.py:511
  217.5 6.8 %fusion.24 = bf16[1024,6,64]{0,2,1:T(8,128)(2,1)} fusion(f32[512,6,64]{0,2,1:T(8,128)S(1)} %copy-done.17, bf16[512,6,64]{0,2,1:T(8,128)(2,1)S(1)} %bitcast.138, f32[6,512,1024]{2,1,0:T(8,128)} %copy-done, f32[6,512]{1,0:T(8,128)S(1)} %log_add_fusion), kind=kOutput, calls=%fused_computation.53 | convolution fusion | flops 409731072 | bytes 14561280 | tf_op jit(solution)/shard_map/hqk,qhd->khd/dot_general | solution.py:524
  224.3 4.8 %copy.84 = bf16[1024,1,1,384]{3,1,2,0:T(2,128)(2,1)} copy(bf16[1024,1,1,384]{0,3,2,1:T(8,128)(2,1)} %bitcast.143) | data formatting | bytes 1572864 | tf_op jit(solution)/shard_map/stack | solution.py:633
  229.1 9.5 %multiply_convert_fusion = bf16[6,512,1024]{2,1,0:T(8,128)(2,1)S(1)} fusion(f32[6,512,1024]{2,1,0:T(8,128)} %get-tuple-element.132, f32[6,512,1024]{2,1,0:T(8,128)} %copy-done, f32[6,512]{1,0:T(8,128)} %get-tuple-element.131, f32[6,512]{1,0:T(8,128)S(1)} %log_add_fusion), kind=kLoop, calls=%fused_computation | loop fusion | flops 12582912 | bytes 31481856 | tf_op jit(solution)/shard_map/convert_element_type | solution.py:515
  238.6 2.8 fusion.37
  241.4 2.2 fusion.25
  243.6 4.8 %copy.83 = bf16[1024,1,1,384]{3,1,2,0:T(2,128)(2,1)} copy(bf16[1024,1,1,384]{0,3,2,1:T(8,128)(2,1)} %bitcast.129) | data formatting | bytes 1572864 | tf_op jit(solution)/shard_map/stack | solution.py:633
  248.4 2.1 pad_maximum_fusion.3
  250.5 4.8 %copy.82 = bf16[1024,1,1,384]{3,1,2,0:T(2,128)(2,1)} copy(bf16[1024,1,1,384]{0,3,2,1:T(8,128)(2,1)} %bitcast.145) | data formatting | bytes 1572864 | tf_op jit(solution)/shard_map/stack | solution.py:633
  255.4 7.0 %pad_maximum_fusion = bf16[1024,3,1,384]{3,1,2,0:T(4,128)(2,1)S(1)} fusion(bf16[1024,1,1,384]{3,1,2,0:T(2,128)(2,1)} %copy.84, bf16[1024,1,1,384]{3,1,2,0:T(2,128)(2,1)} %copy.83, bf16[1024,1,1,384]{3,1,2,0:T(2,128)(2,1)} %copy.82), kind=kLoop, calls=%fused_computation.35 | loop fusion | flops 7077888 | bytes 4718592 | tf_op jit(solution)/shard_map/stack | solution.py:633
  262.4 6.3 %all_to_all.66 = bf16[1024,3,1,384]{3,1,2,0:T(4,128)(2,1)S(1)} all-to-all(bf16[1024,3,1,384]{3,1,2,0:T(4,128)(2,1)S(1)} %pad_maximum_fusion), channel_id=1, replica_groups={{0,1},{2,3},{4,5},{6,7},{8,9},{10,11},{12,13},{14,15},{16,17},{18,19},{..., dimensions={0} | all-to-all | bytes 4718592 | tf_op jit(solution)/shard_map/all_to_all | solution.py:554
  270.4 2.6 reduce.10
  273.0 4.3 copy.86
  277.3 6.8 %multiply_reduce_fusion.3 = (bf16[768]{0:T(1024)(128)(2,1)}, f32[512]{0:T(512)}, f32[512,768]{1,0:T(8,128)}) fusion(f32[512]{0:T(512)S(1)} %copy-done.45, f32[512,1]{1,0:T(8,128)S(1)} %copy-done.12, f32[512,767]{1,0:T(8,128)S(1)} %convert_element_type.138, f32[768]{0:T(1024)S(1)} %copy-done.37, bf16[512,2304]{0,1:T(8,128)(2,1)} %bitcast.147, ...), kind=kOutput, calls=%fused_computation.57 | convolution fusion | flops 1814690560 | bytes 9052672 | tf_op jit(solution)/shard_map/dot_general | solution.py:450
  284.1 4.1 convolution_convert_fusion
  288.3 5.1 %fusion.68 = (f32[512]{0:T(512)S(1)}, f32[512,768]{1,0:T(8,128)}) fusion(f32[768]{0:T(1024)S(1)} %copy-done.51, bf16[3072,768]{1,0:T(8,128)(2,1)S(1)} %bitcast.169, f32[512,3072]{1,0:T(8,128)S(1)} %bitcast.120, f32[3072]{0:T(1024)S(1)} %copy-done.42), kind=kOutput, calls=%fused_computation.147 | convolution fusion | flops 2432433664 | bytes 12600320 | tf_op jit(solution)/shard_map/dot_general | solution.py:440
  296.2 2.6 fusion.23
  298.8 7.7 %collective-permute-start.1 = (bf16[512,767]{1,0:T(8,128)(2,1)}, bf16[512,767]{1,0:T(8,128)(2,1)}, u32[]{:S(2)}, u32[]{:S(2)}) collective-permute-start(bf16[512,767]{1,0:T(8,128)(2,1)} %fusion.23), channel_id=1, source_target_pairs={{0,0},{1,16},{2,2},{3,18},{4,4},{5,20},{6,6},{7,22},{8,8},{9,24},{... | collective-permute-start | bytes 2356232 | tf_op jit(solution)/shard_map/ppermute | solution.py:548
  315.3 8.8 %convolution_convert_fusion.2 = bf16[3072,768]{1,0:T(8,128)(2,1)} fusion(f32[512]{0:T(512)S(1)} %copy-done.49, bf16[512,767]{1,0:T(8,128)(2,1)S(1)} %copy-done.6, f32[512,3072]{1,0:T(8,128)} %copy-done.9, f32[3072]{0:T(1024)S(1)} %copy-done.43), kind=kOutput, calls=%fused_computation.30 | convolution fusion | flops 2435186688 | bytes 11809792 | tf_op jit(solution)/shard_map/dot_general | solution.py:444
  324.1 4.6 %convolution_convert_fusion.1 = bf16[768,3072]{1,0:T(8,128)(2,1)} fusion(bf16[512,3072]{1,0:T(8,128)(2,1)S(1)} %copy-done.56, f32[512,768]{1,0:T(8,128)S(1)} %get-tuple-element.109, f32[768]{0:T(1024)S(1)} %copy-done.31, f32[512]{0:T(512)S(1)} %copy-done.34), kind=kOutput, calls=%fused_computation.29 | convolution fusion | flops 2419458048 | bytes 9442304 | tf_op jit(solution)/shard_map/dot_general | solution.py:444
  328.7 109.2 %scatter_grads.1 = (f32[192,768]{1,0:T(8,128)}, f32[48,3072]{1,0:T(8,128)}, f32[48,768]{1,0:T(8,128)}, f32[48,2304]{1,0:T(8,128)}, f32[16,256]{1,0:T(8,128)}) custom-call(bf16[4,2,2,192,768]{4,3,2,1,0:T(8,128)(2,1)} %bitcast.121, bf16[4,2,2,48,3072]{4,3,2,1,0:T(8,128)(2,1)} %bitcast.122, bf16[4,2,2,48,768]{4,3,2,1,0:T(8,128)(2,1)} %bitcast.151, ...), custom_call_target="tpu_custom_call" | custom-call | tf_op jit(solution)/shard_map/scatter_grads/pallas_call | solution.py:414
  443.0 2.1 copy.111
  (233 shorter events, 60.4 us)
Async XLA Ops:
  0.6 97.9 %collective-permute-start = (bf16[512,767]{1,0:T(8,128)(2,1)}, bf16[512,767]{1,0:T(8,128)(2,1)S(1)}, u32[]{:S(2)}, u32[]{:S(2)}) collective-permute-start(bf16[512,767]{1,0:T(8,128)(2,1)} %bitcast.174), channel_id=1, source_target_pairs={{0,0},{1,16},{2,2},{3,18},{4,4},{5,20},{6,6},{7,22},{8,8},{9,24},{... | collective-permute-start | bytes 2356232 | tf_op jit(solution)/shard_map/ppermute | solution.py:548
  2.4 118.0 %collective-permute-start.2 = (bf16[512,767]{1,0:T(8,128)(2,1)}, bf16[512,767]{1,0:T(8,128)(2,1)S(1)}, u32[]{:S(2)}, u32[]{:S(2)}) collective-permute-start(bf16[512,767]{1,0:T(8,128)(2,1)} %bitcast.175), channel_id=1, source_target_pairs={{0,0},{1,16},{2,2},{3,18},{4,4},{5,20},{6,6},{7,22},{8,8},{9,24},{... | collective-permute-start | bytes 2356232 | tf_op jit(solution)/shard_map/ppermute | solution.py:548
  95.0 9.5 %copy-start.36 = (f32[768]{0:T(1024)}, f32[768]{0:T(1024)S(1)}, u32[]{:S(2)}) copy-start(f32[768]{0:T(1024)S(1)} %mul.213) | copy-start | bytes 9220
  98.8 5.6 %copy-start.10 = (f32[512,1]{1,0:T(8,128)}, f32[512,1]{1,0:T(8,128)S(1)}, u32[]{:S(2)}) copy-start(f32[512,1]{1,0:T(8,128)S(1)} %copy.64) | copy-start | bytes 6148
  99.8 4.7 %copy-start.44 = (f32[512]{0:T(512)}, f32[512]{0:T(512)S(1)}, u32[]{:S(2)}) copy-start(f32[512]{0:T(512)S(1)} %fusion.50) | copy-start | bytes 6148
  120.4 10.7 %copy-start.4 = (bf16[512,767]{1,0:T(8,128)(2,1)}, bf16[512,767]{1,0:T(8,128)(2,1)S(1)}, u32[]{:S(2)}) copy-start(bf16[512,767]{1,0:T(8,128)(2,1)S(1)} %collective-permute-done.2) | copy-start | bytes 2356228
  122.7 14.6 %copy-start.7 = (bf16[1024,1,1,384]{0,3,2,1:T(8,128)(2,1)}, bf16[1024,1,1,384]{0,3,2,1:T(8,128)(2,1)S(1)}, u32[]{:S(2)}) copy-start(bf16[1024,1,1,384]{0,3,2,1:T(8,128)(2,1)S(1)} %copy.73) | copy-start | bytes 2359300
  139.8 4.5 %copy-start = (f32[6,512,1024]{2,1,0:T(8,128)}, f32[6,512,1024]{2,1,0:T(8,128)S(1)}, u32[]{:S(2)}) copy-start(f32[6,512,1024]{2,1,0:T(8,128)S(1)} %get-tuple-element.121) | copy-start | bytes 37748740
  139.8 4.5 %copy-start.16 = (bf16[1024,1,1,384]{0,3,2,1:T(8,128)(2,1)S(1)}, bf16[1024,1,1,384]{0,3,2,1:T(8,128)(2,1)}, u32[]{:S(2)}) copy-start(bf16[1024,1,1,384]{0,3,2,1:T(8,128)(2,1)} %copy.71) | copy-start | bytes 2359300
  162.8 15.4 %copy-start.33 = (f32[512]{0:T(512)}, f32[512]{0:T(512)S(1)}, u32[]{:S(2)}) copy-start(f32[512]{0:T(512)S(1)} %fusion.51) | copy-start | bytes 6148
  165.8 9.1 %copy-start.9 = (f32[512,3072]{1,0:T(8,128)}, f32[512,3072]{1,0:T(8,128)S(1)}, u32[]{:S(2)}) copy-start(f32[512,3072]{1,0:T(8,128)S(1)} %fusion.52) | copy-start | bytes 18874372
  190.0 4.9 %copy-start.13 = (bf16[1,512,1,384]{1,3,2,0:T(8,128)(2,1)S(1)}, bf16[1,512,1,384]{1,3,2,0:T(8,128)(2,1)}, u32[]{:S(2)}) copy-start(bf16[1,512,1,384]{1,3,2,0:T(8,128)(2,1)} %copy.77) | copy-start | bytes 1179652
  190.0 5.0 %copy-start.22 = (bf16[512,1,1,384]{0,3,2,1:T(8,128)(2,1)S(1)}, bf16[512,1,1,384]{0,3,2,1:T(8,128)(2,1)}, u32[]{:S(2)}) copy-start(bf16[512,1,1,384]{0,3,2,1:T(8,128)(2,1)} %copy.67) | copy-start | bytes 1179652
  190.0 5.0 %copy-start.29 = (f32[6,512]{1,0:T(8,128)S(1)}, f32[6,512]{1,0:T(8,128)}, u32[]{:S(2)}) copy-start(f32[6,512]{1,0:T(8,128)} %log_add_fusion.1) | copy-start | bytes 36868
  190.0 9.3 %slice-start = ((s8[6291456]{0:T(1024)(128)(4,1)}), s8[4194304]{0:T(1024)(128)(4,1)S(1)}, s32[]{:S(2)}) async-start(s8[6291456]{0:T(1024)(128)(4,1)} %bitcast.111), calls=%async_computation.4 | async-start | bytes 8388608
  195.0 4.4 slice-start.1
  207.6 9.9 %copy-start.15 = (bf16[1,512,1,384]{1,3,2,0:T(8,128)(2,1)S(1)}, bf16[1,512,1,384]{1,3,2,0:T(8,128)(2,1)}, u32[]{:S(2)}) copy-start(bf16[1,512,1,384]{1,3,2,0:T(8,128)(2,1)} %copy.79) | copy-start | bytes 1179652
  207.6 9.9 %copy-start.17 = (f32[512,6,64]{0,2,1:T(8,128)S(1)}, f32[512,6,64]{0,2,1:T(8,128)}, u32[]{:S(2)}) copy-start(f32[512,6,64]{0,2,1:T(8,128)} %fusion.28) | copy-start | bytes 2359300
  229.1 9.5 %copy-start.8 = (bf16[1024,1,1,384]{0,3,2,1:T(8,128)(2,1)S(1)}, bf16[1024,1,1,384]{0,3,2,1:T(8,128)(2,1)}, u32[]{:S(2)}) copy-start(bf16[1024,1,1,384]{0,3,2,1:T(8,128)(2,1)} %copy-done.7) | copy-start | bytes 2359300
  270.4 6.9 %copy-start.12 = (f32[512,1]{1,0:T(8,128)S(1)}, f32[512,1]{1,0:T(8,128)}, u32[]{:S(2)}) copy-start(f32[512,1]{1,0:T(8,128)} %copy-done.10) | copy-start | bytes 6148
  270.4 6.9 %copy-start.37 = (f32[768]{0:T(1024)S(1)}, f32[768]{0:T(1024)}, u32[]{:S(2)}) copy-start(f32[768]{0:T(1024)} %copy-done.36) | copy-start | bytes 9220
  270.4 6.9 %copy-start.45 = (f32[512]{0:T(512)S(1)}, f32[512]{0:T(512)}, u32[]{:S(2)}) copy-start(f32[512]{0:T(512)} %copy-done.44) | copy-start | bytes 6148
  277.3 6.8 %copy-start.19 = (bf16[512,3,2,1,384]{0,4,2,1,3:T(8,128)(2,1)S(1)}, bf16[512,3,2,1,384]{0,4,2,1,3:T(8,128)(2,1)}, u32[]{:S(2)}) copy-start(bf16[512,3,2,1,384]{0,4,2,1,3:T(8,128)(2,1)} %copy.86) | copy-start | bytes 7077892
  277.3 10.9 %slice-start.2 = ((s8[6291456]{0:T(1024)(128)(4,1)}), s8[4194304]{0:T(1024)(128)(4,1)S(1)}, s32[]{:S(2)}) async-start(s8[6291456]{0:T(1024)(128)(4,1)} %bitcast.119), calls=%async_computation.6 | async-start | bytes 8388608
  277.3 10.9 %slice-start.8 = ((s8[4718592]{0:T(1024)(128)(4,1)}), s8[4194304]{0:T(1024)(128)(4,1)S(1)}, s32[]{:S(2)}) async-start(s8[4718592]{0:T(1024)(128)(4,1)} %bitcast.167), calls=%async_computation.12 | async-start | bytes 8388608
  284.1 4.1 copy-start.51
  284.1 4.1 slice-start.9
  288.3 5.7 %copy-start.47 = (bf16[768]{0:T(1024)(128)(2,1)S(1)}, bf16[768]{0:T(1024)(128)(2,1)}, u32[]{:S(2)}) copy-start(bf16[768]{0:T(1024)(128)(2,1)} %get-tuple-element.104) | copy-start | bytes 4612
  288.3 6.4 %copy-start.52 = (bf16[768]{0:T(1024)(128)(2,1)S(1)}, bf16[768]{0:T(1024)(128)(2,1)}, u32[]{:S(2)}) copy-start(bf16[768]{0:T(1024)(128)(2,1)} %get-tuple-element.96) | copy-start | bytes 4612
  288.3 7.1 %copy-start.46 = (bf16[768]{0:T(1024)(128)(2,1)S(1)}, bf16[768]{0:T(1024)(128)(2,1)}, u32[]{:S(2)}) copy-start(bf16[768]{0:T(1024)(128)(2,1)} %get-tuple-element.136) | copy-start | bytes 4612
  288.3 7.7 %copy-start.50 = (bf16[3072]{0:T(1024)(128)(2,1)S(1)}, bf16[3072]{0:T(1024)(128)(2,1)}, u32[]{:S(2)}) copy-start(bf16[3072]{0:T(1024)(128)(2,1)} %get-tuple-element.134) | copy-start | bytes 18436
  296.1 12.3 %copy-start.3 = (f32[512,768]{1,0:T(8,128)S(1)}, f32[512,768]{1,0:T(8,128)}, u32[]{:S(2)}) copy-start(f32[512,768]{1,0:T(8,128)} %copy-done.2) | copy-start | bytes 4718596
  296.1 12.3 %copy-start.23 = (f32[512,768]{1,0:T(8,128)S(1)}, f32[512,768]{1,0:T(8,128)}, u32[]{:S(2)}) copy-start(f32[512,768]{1,0:T(8,128)} %get-tuple-element.133) | copy-start | bytes 4718596
  298.8 144.2 %collective-permute-start.1 = (bf16[512,767]{1,0:T(8,128)(2,1)}, bf16[512,767]{1,0:T(8,128)(2,1)}, u32[]{:S(2)}, u32[]{:S(2)}) collective-permute-start(bf16[512,767]{1,0:T(8,128)(2,1)} %fusion.23), channel_id=1, source_target_pairs={{0,0},{1,16},{2,2},{3,18},{4,4},{5,20},{6,6},{7,22},{8,8},{9,24},{... | collective-permute-start | bytes 2356232 | tf_op jit(solution)/shard_map/ppermute | solution.py:548
  308.5 4.1 copy-start.40
  308.5 4.2 copy-start.38
  308.5 4.2 copy-start.39
  309.7 5.6 %copy-start.6 = (bf16[512,767]{1,0:T(8,128)(2,1)S(1)}, bf16[512,767]{1,0:T(8,128)(2,1)}, u32[]{:S(2)}) copy-start(bf16[512,767]{1,0:T(8,128)(2,1)} %copy-done.4) | copy-start | bytes 2356228
  309.7 5.6 %copy-start.43 = (f32[3072]{0:T(1024)S(1)}, f32[3072]{0:T(1024)}, u32[]{:S(2)}) copy-start(f32[3072]{0:T(1024)} %reshape.359) | copy-start | bytes 36868
  309.7 5.6 %copy-start.49 = (f32[512]{0:T(512)S(1)}, f32[512]{0:T(512)}, u32[]{:S(2)}) copy-start(f32[512]{0:T(512)} %broadcast_multiply_fusion.1) | copy-start | bytes 6148
  312.7 130.3 %collective-permute-start.3 = (bf16[512,767]{1,0:T(8,128)(2,1)}, bf16[512,767]{1,0:T(8,128)(2,1)S(1)}, u32[]{:S(2)}, u32[]{:S(2)}) collective-permute-start(bf16[512,767]{1,0:T(8,128)(2,1)} %fusion.22), channel_id=1, source_target_pairs={{0,0},{1,16},{2,2},{3,18},{4,4},{5,20},{6,6},{7,22},{8,8},{9,24},{... | collective-permute-start | bytes 2356232 | tf_op jit(solution)/shard_map/ppermute | solution.py:548
  315.3 8.8 %copy-start.31 = (f32[768]{0:T(1024)S(1)}, f32[768]{0:T(1024)}, u32[]{:S(2)}) copy-start(f32[768]{0:T(1024)} %mul.221) | copy-start | bytes 9220
  315.3 8.8 %copy-start.34 = (f32[512]{0:T(512)S(1)}, f32[512]{0:T(512)}, u32[]{:S(2)}) copy-start(f32[512]{0:T(512)} %copy-done.33) | copy-start | bytes 6148
  315.3 8.8 %copy-start.56 = (bf16[512,3072]{1,0:T(8,128)(2,1)S(1)}, bf16[512,3072]{1,0:T(8,128)(2,1)}, u32[]{:S(2)}) copy-start(bf16[512,3072]{1,0:T(8,128)(2,1)} %copy-done.55) | copy-start | bytes 9437188
  437.9 8.1 %copy-start.28 = (f32[48,2304]{1,0:T(8,128)S(1)}, f32[48,2304]{1,0:T(8,128)}, u32[]{:S(2)}) copy-start(f32[48,2304]{1,0:T(8,128)} %get-tuple-element.149) | copy-start | bytes 1327108
  437.9 8.8 %copy-start.32 = (f32[48,768]{1,0:T(8,128)S(1)}, f32[48,768]{1,0:T(8,128)}, u32[]{:S(2)}) copy-start(f32[48,768]{1,0:T(8,128)} %get-tuple-element.150) | copy-start | bytes 442372
  437.9 9.5 %copy-start.27 = (f32[48,3072]{1,0:T(8,128)S(1)}, f32[48,3072]{1,0:T(8,128)}, u32[]{:S(2)}) copy-start(f32[48,3072]{1,0:T(8,128)} %get-tuple-element.151) | copy-start | bytes 1769476
  437.9 10.3 %copy-start.26 = (f32[192,768]{1,0:T(8,128)S(1)}, f32[192,768]{1,0:T(8,128)}, u32[]{:S(2)}) copy-start(f32[192,768]{1,0:T(8,128)} %get-tuple-element.152) | copy-start | bytes 1769476
  (23 other events, 58.0 us)
